TPU v7x, 32 devices: a whole 2x2x4 slice. The times are simulated.
32 devices in a mesh: groups: 2 (over x), date: 16 (over z, y, core).
Axes of the slice: x: 2, y: 2, z: 4, core: 2. Of those that a mesh axis runs over, the one named last changes fastest.
Arguments:
- images: float32 [32, 2, 64, 2560], P(('groups', 'date')), parts along dimension 0, may hold values from -16 to 16
- height_phase: float32 [128, 2560], P(('groups', 'date')), parts along dimension 0, may hold values from -4 to 4
- baseline: float32 [32], P('groups'), parts along dimension 0, may hold values from -0.6 to 0.6
- pair_list: int32 [32, 2], replicated, may hold values from 0 to 15, as said below
- pair_owner: int32 [32, 1], replicated, may hold values from 0 to 15; in each aligned block of 32 rows (0 to 31, 32 to 63, ...) at most 4 rows name the same one
Outputs:
- interferogram: float32 [128, 2, 16, 128], P(('groups', 'date')), parts along dimension 0
- coherence: float32 [128, 16, 128], P(('groups', 'date')), parts along dimension 0
There are 2 independent parts, one for each index of `groups`. A program takes and returns all parts, laid end to end along the dimension named above; an argument that names none is the same for every part. Nothing has to cross between parts.
Inputs may be any that keep to these rules, and one draw needn't show every extreme that they name: `pair_list`: each row is (r, s) with r < s <= r + 4; some pair has s = r + 4. `pair_owner`: every index owns at least one pair and at most 4 pairs; some index owns exactly 4.
All inputs are finite; a program needn't handle non-finite values.
Results may differ from a plain program's by a relative error of at most 0.00007.
Values sent between devices are 32-bit elements; how exact they have to be, the bound alone decides.
A program may use at most 128 MiB of HBM per device.

v0:
```python
import functools
import math

import jax
import jax.numpy as jnp
from jax import lax
from jax.experimental import pallas as pl
from jax.experimental.pallas import tpu as pltpu
from jax.sharding import PartitionSpec as P

LOOK_ROWS = 4
LOOK_COLS = 20
CAP = 4
BAND = 4
EPSILON = 1e-06
LANES = 128
TILE = 8
LAG = 5
AHEAD = 8


def split(values, parts):
    pieces = []
    for _ in range(parts):
        piece = values.astype(jnp.bfloat16)
        pieces.append(piece)
        values = values - piece.astype(jnp.float32)
    return pieces


def cos_sin(angle):
    square = angle * angle
    sine = jnp.full_like(angle, -1.0 / math.factorial(15))
    for term in range(6, -1, -1):
        sine = sine * square + (-1.0) ** term / math.factorial(2 * term + 1)
    cosine = jnp.full_like(angle, 1.0 / math.factorial(16))
    for term in range(7, -1, -1):
        cosine = cosine * square + (-1.0) ** term / math.factorial(2 * term)
    return cosine, sine * angle


def kernel(
    devices, images, height, baseline, pair_list, pair_owner, looks_out, coherence_out,
    window, heights, box, sums, pick_look, pick_first, pick_second,
    stack_real, stack_imag, stack_power, outbox, inbox,
    plane_send, relay_send, plane_recv, relay_recv, height_send, height_recv, out_send, out_recv,
):
    me = lax.axis_index("date")
    planes = devices // BAND
    plane = lax.div(me, BAND)
    spot = lax.rem(me, BAND)
    rows, columns = images.shape[1:]
    blocks = columns // LANES
    tiles = rows // (2 * BAND * TILE)
    chunks = tiles * blocks
    side = BAND * TILE
    sources = devices // BAND
    look_rows = TILE // LOOK_ROWS

    def peer(step):
        return lax.rem(me + step, devices)

    barrier = pltpu.get_barrier_semaphore()

    @pl.loop(1, devices)
    def _(step):
        pl.semaphore_signal(barrier, inc=1, device_id={"date": peer(step)})

    pl.semaphore_wait(barrier, devices - 1)

    def lines(quarter, upper, chunk):
        first = ((quarter * 2 + upper) * tiles + lax.div(chunk, blocks)) * TILE
        column = lax.rem(chunk, blocks) * LANES
        return images.at[
            :, pl.ds(pl.multiple_of(first, TILE), TILE), pl.ds(pl.multiple_of(column, LANES), LANES)
        ]

    def place(upper, chunk, slot, size=TILE):
        return window.at[upper, chunk, :, pl.ds(pl.multiple_of(slot * TILE, TILE), size), :]

    def own_slot(upper, which):
        return (1 - upper) * BAND + which

    def plane_copy(step, upper, chunk):
        to = spot ^ step
        return pltpu.make_async_remote_copy(
            src_ref=lines(to, upper, chunk),
            dst_ref=place(upper, chunk, own_slot(upper, spot)),
            send_sem=plane_send.at[upper, chunk],
            recv_sem=plane_recv.at[upper, chunk, spot],
            device_id={"date": plane * BAND + to},
        )

    def plane_arrival(step, upper, chunk):
        source = spot ^ step
        return pltpu.make_async_remote_copy(
            src_ref=lines(source, upper, chunk),
            dst_ref=place(upper, chunk, own_slot(upper, source)),
            send_sem=plane_send.at[upper, chunk],
            recv_sem=plane_recv.at[upper, chunk, source],
            device_id={"date": plane * BAND + source},
        )

    def own_copy(upper, chunk):
        return pltpu.make_async_copy(
            lines(spot, upper, chunk),
            place(upper, chunk, own_slot(upper, spot)),
            plane_recv.at[upper, chunk, spot],
        )

    def relays(upper):
        return plane < planes - 1 if upper == 0 else plane > 0

    def gets_relays(upper):
        return plane > 0 if upper == 0 else plane < planes - 1

    def relay_copy(upper, chunk, which, source):
        return pltpu.make_async_remote_copy(
            src_ref=source,
            dst_ref=place(upper, chunk, upper * BAND + which),
            send_sem=relay_send.at[upper, chunk],
            recv_sem=relay_recv.at[upper, chunk],
            device_id={"date": me + BAND * (1 - 2 * upper)},
        )

    def relay_all(upper, chunk):
        return pltpu.make_async_remote_copy(
            src_ref=place(upper, chunk, (1 - upper) * BAND, side),
            dst_ref=place(upper, chunk, upper * BAND, side),
            send_sem=relay_send.at[upper, chunk],
            recv_sem=relay_recv.at[upper, chunk],
            device_id={"date": me},
        )

    def plane_all(upper, chunk):
        return pltpu.make_async_remote_copy(
            src_ref=place(upper, chunk, 0, side - TILE),
            dst_ref=place(upper, chunk, 0, side - TILE),
            send_sem=plane_send.at[upper, chunk],
            recv_sem=relay_recv.at[upper, chunk],
            device_id={"date": me},
        )

    reader = lax.div(me, sources)
    own_height = lax.rem(me, sources)

    def height_copy(to_plane):
        return pltpu.make_async_remote_copy(
            src_ref=height,
            dst_ref=heights.at[own_height],
            send_sem=height_send.at[to_plane],
            recv_sem=height_recv.at[own_height],
            device_id={"date": to_plane * BAND + reader},
        )

    def height_own():
        return pltpu.make_async_copy(height, heights.at[own_height], height_recv.at[own_height])

    def height_arrival(source):
        return pltpu.make_async_remote_copy(
            src_ref=height,
            dst_ref=heights.at[source],
            send_sem=height_send.at[0],
            recv_sem=height_recv.at[source],
            device_id={"date": me},
        )

    @pl.loop(0, planes)
    def _(to_plane):
        @pl.when(to_plane * BAND + reader != me)
        def _():
            height_copy(to_plane).start()

        @pl.when(to_plane * BAND + reader == me)
        def _():
            height_own().start()

    @pl.loop(0, chunks)
    def _(chunk):
        for upper in range(2):
            for step in (2, 3, 1):
                plane_copy(step, upper, chunk).start()

            @pl.when(relays(upper))
            def _():
                relay_copy(upper, chunk, spot, lines(spot, upper, chunk)).start()

            own_copy(upper, chunk).start()

    for upper in range(2):
        @pl.when(jnp.logical_not(gets_relays(upper)))
        def _():
            @pl.loop(0, chunks)
            def _(chunk):
                window[upper, chunk, :, upper * side:(upper + 1) * side, :] = jnp.zeros(
                    (2, side, LANES), jnp.float32
                )

    position = lax.broadcasted_iota(jnp.int32, (columns, LANES), 0)
    target = lax.broadcasted_iota(jnp.int32, (columns, LANES), 1) * LOOK_COLS
    box[...] = jnp.where(
        (position >= target) & (position < target + LOOK_COLS), 1.0, 0.0
    ).astype(jnp.bfloat16)
    sums[...] = jnp.zeros_like(sums)

    dates = 2 * BAND
    lane = lax.broadcasted_iota(jnp.int32, (dates, devices), 1)
    date = lax.broadcasted_iota(jnp.int32, (dates, devices), 0)
    scales = []
    for upper in range(2):
        chosen_date = lane == date + (plane - 1 + upper) * BAND
        scales.append(
            jnp.sum(jnp.where(chosen_date, baseline[...], 0.0), axis=1, keepdims=True)
        )

    owner = pair_owner[...].astype(jnp.float32)
    pairs = owner.shape[1]
    down = lax.broadcasted_iota(jnp.int32, (pairs, pairs), 0)
    across = lax.broadcasted_iota(jnp.int32, (pairs, pairs), 1)
    owner_column = jnp.sum(jnp.where(down == across, owner, 0.0), axis=1, keepdims=True)
    earlier = (owner_column == owner) & (down < across)
    spot_of = owner * TILE + jnp.sum(jnp.where(earlier, 1.0, 0.0), axis=0, keepdims=True)
    first = pair_list[0:1, :]
    second = pair_list[1:2, :]
    total = devices * TILE
    line = lax.broadcasted_iota(jnp.int32, (total, pairs), 0)
    taken = (line - (line & CAP)).astype(jnp.float32) == spot_of

    def pick(value, valid, size):
        lane = lax.broadcasted_iota(jnp.int32, (total, 3 * size), 1) & (size - 1)
        listed = jnp.sum(
            jnp.where(taken & valid, value.astype(jnp.float32) + 1.0, 0.0), axis=1, keepdims=True
        ) - 1.0
        return jnp.where(lane.astype(jnp.float32) == listed, 1.0, 0.0).astype(jnp.bfloat16)

    for upper in range(2):
        ends_here = second if upper == 0 else first
        valid = (ends_here >= plane * BAND) & (ends_here < (plane + 1) * BAND)
        start = first - (plane - 1 + upper) * BAND
        distance = second - first
        pick_look[upper] = pick((distance - 1) * dates + start, valid, BAND * dates)
        pick_first[upper] = pick(start, valid, dates)
        pick_second[upper] = pick(start + distance, valid, dates)

    def forward(chunk):
        for upper in range(2):
            own_copy(upper, chunk).wait()
        for step in (1, 2, 3):
            for upper in range(2):
                plane_arrival(step, upper, chunk).wait_recv()

                @pl.when(relays(upper))
                def _():
                    which = spot ^ step
                    relay_copy(
                        upper, chunk, which, place(upper, chunk, own_slot(upper, which))
                    ).start()

    def compute(chunk):
        for upper in range(2):
            @pl.when(gets_relays(upper))
            def _():
                relay_all(upper, chunk).wait_recv()

        tile = lax.div(chunk, blocks)
        column = pl.multiple_of(lax.rem(chunk, blocks) * LANES, LANES)
        totals = []
        for upper in range(2):
            for look_row in range(look_rows):
                found = [None] * (1 + 2 * BAND)

                def add(at, value):
                    found[at] = value if found[at] is None else found[at] + value

                source = (upper * tiles + tile) * look_rows + look_row
                for row in range(LOOK_ROWS):
                    level = heights[source, row:row + 1, pl.ds(column, LANES)]
                    cosine, sine = cos_sin(scales[upper] * level)
                    at = pl.ds(look_row * LOOK_ROWS + row, dates, stride=TILE)
                    real = window[upper, chunk, 0, at, :]
                    imag = window[upper, chunk, 1, at, :]
                    flat_real = real * cosine - imag * sine
                    flat_imag = real * sine + imag * cosine
                    add(0, flat_real * flat_real + flat_imag * flat_imag)
                    for distance in range(1, BAND + 1):
                        next_real = pltpu.roll(flat_real, dates - distance, 0)
                        next_imag = pltpu.roll(flat_imag, dates - distance, 0)
                        add(distance, flat_real * next_real + flat_imag * next_imag)
                        add(BAND + distance, flat_imag * next_real - flat_real * next_imag)
                totals.extend(found)
        weights = box[pl.ds(column, LANES), :]
        summed = sums[tile]
        for piece in split(jnp.concatenate(totals, axis=0), 2):
            summed = summed + jnp.dot(piece, weights, preferred_element_type=jnp.float32)
        sums[tile] = summed

    @pl.loop(0, AHEAD)
    def _(chunk):
        forward(chunk)

    @pl.loop(0, sources)
    def _(source):
        height_arrival(source).wait_recv()

    @pl.loop(0, AHEAD - LAG)
    def _(chunk):
        compute(chunk)

    @pl.loop(AHEAD, chunks)
    def _(chunk):
        forward(chunk)
        compute(chunk - LAG)

    @pl.loop(chunks - LAG, chunks)
    def _(chunk):
        compute(chunk)

    def chosen(pick_matrix, stack):
        return jnp.dot(pick_matrix, stack[...], preferred_element_type=jnp.float32)

    kind = lax.broadcasted_iota(jnp.int32, (total, LANES), 0) & CAP
    quantities = (1 + 2 * BAND) * dates
    ends = (0, dates, (1 + BAND) * dates, quantities)
    for tile in range(tiles):
        mean = sums[tile] * (1.0 / (LOOK_ROWS * LOOK_COLS))
        for upper in range(2):
            ratios = []
            for look_row in range(look_rows):
                base = (upper * look_rows + look_row) * quantities
                for stack, low, high in zip((stack_power, stack_real, stack_imag), ends[:-1], ends[1:]):
                    size = high - low
                    stack[...] = jnp.concatenate(
                        [p.astype(jnp.float32) for p in split(mean[base + low:base + high], 3)], axis=0
                    ).astype(jnp.bfloat16)
                look_real = chosen(pick_look[upper], stack_real)
                look_imag = chosen(pick_look[upper], stack_imag)
                denominator = jnp.sqrt(
                    (chosen(pick_first[upper], stack_power) + EPSILON)
                    * (chosen(pick_second[upper], stack_power) + EPSILON)
                )
                ratios.append(jnp.sqrt(look_real * look_real + look_imag * look_imag) / denominator)
                outbox[(tile * 2 + upper) * 3 + look_row] = jnp.where(kind == 0, look_real, look_imag)
            outbox[(tile * 2 + upper) * 3 + 2] = jnp.where(kind == 0, ratios[0], ratios[1])

    def parcel(which):
        return pl.ds(pl.multiple_of(which * TILE, TILE), TILE)

    def out_copy(to):
        return pltpu.make_async_remote_copy(
            src_ref=outbox.at[:, parcel(to), :],
            dst_ref=inbox.at[me],
            send_sem=out_send.at[to],
            recv_sem=out_recv.at[me],
            device_id={"date": to},
        )

    def out_arrival(source):
        return pltpu.make_async_remote_copy(
            src_ref=outbox.at[:, parcel(source), :],
            dst_ref=inbox.at[source],
            send_sem=out_send.at[source],
            recv_sem=out_recv.at[source],
            device_id={"date": source},
        )

    @pl.loop(1, devices)
    def _(step):
        out_copy(peer(step)).start()

    inbox[me] = outbox[:, parcel(me), :]

    @pl.loop(0, planes)
    def _(to_plane):
        @pl.when(to_plane * BAND + reader != me)
        def _():
            height_copy(to_plane).wait_send()

    @pl.loop(0, chunks)
    def _(chunk):
        for upper in range(2):
            plane_all(upper, chunk).wait_send()

            @pl.when(relays(upper))
            def _():
                relay_all(upper, chunk).wait_send()

    @pl.loop(1, devices)
    def _(step):
        out_arrival(peer(step)).wait_recv()

    height_rows = 2 * tiles * look_rows * BAND
    for quarter in range(BAND):
        for tile in range(tiles):
            for upper in range(2):
                for part in range(3):
                    value = inbox[quarter, (tile * 2 + upper) * 3 + part]
                    for other in range(1, planes):
                        value = value + inbox[other * BAND + quarter, (tile * 2 + upper) * 3 + part]
                    row = ((quarter * 2 + upper) * tiles + tile) * look_rows
                    for c in range(2):
                        piece = value[c * CAP:(c + 1) * CAP]
                        if part < 2:
                            looks_out[pl.ds(c * height_rows + row + part, CAP, stride=2 * height_rows), :] = piece
                        else:
                            coherence_out[pl.ds(row + c, CAP, stride=height_rows), :] = piece

    @pl.loop(1, devices)
    def _(step):
        out_copy(peer(step)).wait_send()


def body(images, height_phase, baseline, pair_list, pair_owner):
    devices = lax.axis_size("date")
    rows, columns = images.shape[2:]
    lanes = columns // LOOK_COLS
    looks = rows // LOOK_ROWS
    tiles = rows // (2 * BAND * TILE)
    chunks = tiles * (columns // LANES)
    dates = 2 * BAND
    assert lanes == LANES and rows == LOOK_ROWS * devices and TILE == 2 * LOOK_ROWS
    assert rows % (2 * BAND * TILE) == 0 and columns % LANES == 0
    quantities = 1 + 2 * BAND
    total = devices * TILE
    vmem = pl.BlockSpec(memory_space=pltpu.VMEM)
    hbm = pl.BlockSpec(memory_space=pltpu.HBM)
    look, coherence = pl.pallas_call(
        functools.partial(kernel, devices),
        out_shape=(
            jax.ShapeDtypeStruct((CAP * 2 * looks, lanes), jnp.float32),
            jax.ShapeDtypeStruct((CAP * looks, lanes), jnp.float32),
        ),
        in_specs=[hbm, hbm, vmem, vmem, vmem],
        out_specs=(vmem, vmem),
        scratch_shapes=[
            pltpu.VMEM((2, chunks, 2, dates * TILE, LANES), jnp.float32),
            pltpu.VMEM((devices // BAND, LOOK_ROWS, columns), jnp.float32),
            pltpu.VMEM((columns, lanes), jnp.bfloat16),
            pltpu.VMEM((tiles, 4 * quantities * dates, lanes), jnp.float32),
            pltpu.VMEM((2, total, 3 * BAND * dates), jnp.bfloat16),
            pltpu.VMEM((2, total, 3 * dates), jnp.bfloat16),
            pltpu.VMEM((2, total, 3 * dates), jnp.bfloat16),
            pltpu.VMEM((3 * BAND * dates, lanes), jnp.bfloat16),
            pltpu.VMEM((3 * BAND * dates, lanes), jnp.bfloat16),
            pltpu.VMEM((3 * dates, lanes), jnp.bfloat16),
            pltpu.VMEM((tiles * 6, total, lanes), jnp.float32),
            pltpu.VMEM((devices, tiles * 6, TILE, lanes), jnp.float32),
            pltpu.SemaphoreType.DMA((2, chunks)),
            pltpu.SemaphoreType.DMA((2, chunks)),
            pltpu.SemaphoreType.DMA((2, chunks, BAND)),
            pltpu.SemaphoreType.DMA((2, chunks)),
            pltpu.SemaphoreType.DMA((devices // BAND,)),
            pltpu.SemaphoreType.DMA((devices // BAND,)),
            pltpu.SemaphoreType.DMA((devices,)),
            pltpu.SemaphoreType.DMA((devices,)),
        ],
        compiler_params=pltpu.CompilerParams(
            collective_id=0, has_side_effects=True
        ),
    )(images[0], height_phase, baseline[None], pair_list.T, pair_owner.T)
    return look.reshape(CAP, 2, looks, lanes), coherence.reshape(CAP, looks, lanes)


def solution(mesh):
    in_specs = (
        P(("groups", "date"), None, None, None),
        P(("groups", "date"), None),
        P("groups"),
        P(),
        P(),
    )
    out_specs = (P(("groups", "date"), None, None, None), P(("groups", "date"), None, None))
    return jax.shard_map(body, mesh=mesh, in_specs=in_specs, out_specs=out_specs, check_vma=False)
```

profile of v0, /device:TPU:1, one launch (start us, length us, event | category | flops | bytes accessed | tf_op | source)
XLA Modules:
  0.0 42.2 jit_solution(11864283690490009236)
XLA Ops:
  0.6 38.8 %shard_map.68 = (f32[128,128]{1,0:T(8,128)}, f32[64,128]{1,0:T(8,128)}) custom-call(f32[2,64,2560]{2,1,0:T(8,128)} %bitcast.6, f32[4,2560]{1,0:T(4,128)} %height.1, f32[1,16]{1,0:T(1,128)} %bitcast.10, s32[2,32]{1,0:T(2,128)} %bitcast.9, s32[1,32]{1,0:T(1,128)} %bitcast.11), custom_call_target="tpu_custom_call" | custom-call | tf_op jit(solution)/shard_map/pallas_call | solution.py:426
  39.4 1.5 %copy.9 = f32[4,2,16,128]{3,2,1,0:T(8,128)} copy(f32[4,2,16,128]{3,2,1,0:T(8,128)} %bitcast.7) | data formatting | bytes 131072
  40.9 1.4 %copy.10 = f32[4,16,128]{2,1,0:T(8,128)} copy(f32[4,16,128]{2,1,0:T(8,128)} %bitcast.8) | data formatting | bytes 65536
where the time goes:
time: 42.9 us; the launch traced here: 42.2 us
  Pallas kernels  38.8 us (90%)
  local copies, waits for them, and re-layouts  2.85 us (7%)
  between operations  0.64 us (1%)
    pallas_call x1, Pallas kernels, body(): pl.pallas_call(functools.partial(kernel, devices), out_shape=(jax.ShapeDt...  38.8 us
    unnamed x2, local copies, waits for them, and re-layouts  2.85 us

commit v1 on v0

v1 whole, which is shorter than its diff:
```python
import functools
import math

import jax
import jax.numpy as jnp
from jax import lax
from jax.experimental import pallas as pl
from jax.experimental.pallas import tpu as pltpu
from jax.sharding import PartitionSpec as P

LOOK_ROWS = 4
LOOK_COLS = 20
CAP = 4
BAND = 4
EPSILON = 1e-06
LANES = 128
TILE = 8
HALVES = 2
WIDE = 2
QUANTITIES = 2 + 2 * BAND
UNIT = QUANTITIES * TILE
PIECES = 3
DEPTH = 256
AHEAD = 3
FIRST = 2
START = 6
LAG = 5


def split(values, parts):
    pieces = []
    for _ in range(parts):
        piece = values.astype(jnp.bfloat16)
        pieces.append(piece)
        values = values - piece.astype(jnp.float32)
    return pieces


def cos_sin(angle):
    square = angle * angle
    sine = jnp.full_like(angle, -1.0 / math.factorial(15))
    for term in range(6, -1, -1):
        sine = sine * square + (-1.0) ** term / math.factorial(2 * term + 1)
    cosine = jnp.full_like(angle, 1.0 / math.factorial(16))
    for term in range(7, -1, -1):
        cosine = cosine * square + (-1.0) ** term / math.factorial(2 * term)
    return cosine, sine * angle


def kernel(
    devices, phases, images, height, baseline_in, pair_list_in, pair_owner_in, looks_out, coherence_out,
    window, heights, box, sums, picks, stack, chosen, outbox, inbox, baseline, pair_list, pair_owner,
    far, small_sem, plane_send, relay_send, plane_recv, relay_recv, height_send, height_recv, out_send, out_recv,
):
    me = lax.axis_index("date")
    planes = devices // BAND
    plane = lax.div(me, BAND)
    spot = lax.rem(me, BAND)
    tiles = phases // HALVES
    column_tiles = images.shape[2]
    columns = column_tiles * LANES
    part_columns = columns // HALVES
    steps = part_columns // (LANES * WIDE)
    chunks = phases * steps
    side = BAND * TILE
    dates = 2 * BAND
    part_lanes = LANES // HALVES
    look_rows = TILE // LOOK_ROWS
    below, above = plane > 0, plane < planes - 1

    barrier = pltpu.get_barrier_semaphore()

    def hello(to):
        pl.semaphore_signal(barrier, inc=1, device_id={"date": to})

    for step in range(1, BAND):
        hello(plane * BAND + (spot ^ step))

    @pl.when(below)
    def _():
        hello(me - BAND)

    @pl.when(above)
    def _():
        hello(me + BAND)

    reader = lax.div(me, planes)
    own_height = lax.rem(me, planes)

    def small_copies():
        return [
            pltpu.make_async_copy(source, to, small_sem.at[at])
            for at, (source, to) in enumerate(
                ((baseline_in, baseline), (pair_list_in, pair_list), (pair_owner_in, pair_owner))
            )
        ]

    def height_copy(to_plane):
        return pltpu.make_async_remote_copy(
            src_ref=height,
            dst_ref=heights.at[own_height],
            send_sem=height_send.at[to_plane],
            recv_sem=height_recv.at[own_height],
            device_id={"date": to_plane * BAND + reader},
        )

    def height_own():
        return pltpu.make_async_copy(height, heights.at[own_height], height_recv.at[own_height])

    def height_arrival(source):
        return pltpu.make_async_remote_copy(
            src_ref=height,
            dst_ref=heights.at[source],
            send_sem=height_send.at[0],
            recv_sem=height_recv.at[source],
            device_id={"date": me},
        )

    def lines(quarter, upper, chunk):
        phase = lax.div(chunk, steps)
        tile = (quarter * 2 + upper) * tiles + lax.div(phase, HALVES)
        column = lax.rem(phase, HALVES) * (steps * WIDE) + lax.rem(chunk, steps) * WIDE
        return images.at[:, tile, pl.ds(column, WIDE)]

    def place(upper, chunk, slot, size=TILE):
        return window.at[upper, chunk, :, :, pl.ds(pl.multiple_of(slot * TILE, TILE), size), :]

    def own_slot(upper, which):
        return (1 - upper) * BAND + which

    def plane_copy(step, upper, chunk):
        to = spot ^ step
        return pltpu.make_async_remote_copy(
            src_ref=lines(to, upper, chunk),
            dst_ref=place(upper, chunk, own_slot(upper, spot)),
            send_sem=plane_send.at[upper, chunk],
            recv_sem=plane_recv.at[upper, chunk, spot],
            device_id={"date": plane * BAND + to},
        )

    def plane_arrival(step, upper, chunk):
        source = spot ^ step
        return pltpu.make_async_remote_copy(
            src_ref=lines(source, upper, chunk),
            dst_ref=place(upper, chunk, own_slot(upper, source)),
            send_sem=plane_send.at[upper, chunk],
            recv_sem=plane_recv.at[upper, chunk, source],
            device_id={"date": plane * BAND + source},
        )

    def own_copy(upper, chunk):
        return pltpu.make_async_copy(
            lines(spot, upper, chunk),
            place(upper, chunk, own_slot(upper, spot)),
            plane_recv.at[upper, chunk, spot],
        )

    relays = (above, below)
    gets_relays = (below, above)

    def relay_copy(upper, chunk, which, source):
        return pltpu.make_async_remote_copy(
            src_ref=source,
            dst_ref=place(upper, chunk, upper * BAND + which),
            send_sem=relay_send.at[upper, chunk],
            recv_sem=relay_recv.at[upper, chunk],
            device_id={"date": me + BAND * (1 - 2 * upper)},
        )

    def relay_all(upper, chunk):
        return pltpu.make_async_remote_copy(
            src_ref=place(upper, chunk, (1 - upper) * BAND, side),
            dst_ref=place(upper, chunk, upper * BAND, side),
            send_sem=relay_send.at[upper, chunk],
            recv_sem=relay_recv.at[upper, chunk],
            device_id={"date": me},
        )

    def plane_all(upper, chunk):
        return pltpu.make_async_remote_copy(
            src_ref=place(upper, chunk, 0, side - TILE),
            dst_ref=place(upper, chunk, 0, side - TILE),
            send_sem=plane_send.at[upper, chunk],
            recv_sem=relay_recv.at[upper, chunk],
            device_id={"date": me},
        )

    def own_relays(chunk):
        for upper in range(2):
            @pl.when(relays[upper])
            def _():
                relay_copy(upper, chunk, spot, lines(spot, upper, chunk)).start()

    for copy in small_copies():
        copy.start()
    pl.semaphore_wait(barrier, BAND - 1 + jnp.where(below, 1, 0) + jnp.where(above, 1, 0))

    def rows_out(chunk):
        for step in (2, 3, 1):
            for upper in range(2):
                plane_copy(step, upper, chunk).start()
        for upper in range(2):
            own_copy(upper, chunk).start()

    @pl.loop(0, FIRST)
    def _(chunk):
        rows_out(chunk)

    @pl.loop(0, AHEAD)
    def _(chunk):
        own_relays(chunk)

    for turn in range(planes - 1):
        @pl.when(below)
        def _():
            pl.semaphore_signal(far.at[turn], inc=1, device_id={"date": me - BAND})

        @pl.when(above)
        def _():
            pl.semaphore_signal(far.at[turn], inc=1, device_id={"date": me + BAND})

        pl.semaphore_wait(far.at[turn], jnp.where(below, 1, 0) + jnp.where(above, 1, 0))

    @pl.loop(0, planes)
    def _(to_plane):
        @pl.when(to_plane * BAND + reader != me)
        def _():
            height_copy(to_plane).start()

        @pl.when(to_plane * BAND + reader == me)
        def _():
            height_own().start()

    @pl.loop(FIRST, chunks)
    def _(chunk):
        rows_out(chunk)

    for upper in range(2):
        @pl.when(jnp.logical_not(gets_relays[upper]))
        def _():
            @pl.loop(0, chunks)
            def _(chunk):
                window[upper, chunk, :, :, upper * side:(upper + 1) * side, :] = jnp.zeros(
                    (2, WIDE, side, LANES), jnp.float32
                )

    @pl.loop(0, steps * WIDE)
    def _(block):
        shape = (look_rows * LANES, LANES)
        line = lax.broadcasted_iota(jnp.int32, shape, 0)
        position = block * LANES + (line & (LANES - 1))
        target = lax.broadcasted_iota(jnp.int32, shape, 1) - jnp.where(line >= LANES, part_lanes, 0)
        target = target * LOOK_COLS
        box[pl.ds(pl.multiple_of(block * look_rows * LANES, look_rows * LANES), look_rows * LANES), :] = jnp.where(
            (position >= target) & (position < target + LOOK_COLS), 1.0, 0.0
        ).astype(jnp.bfloat16)

    sums[...] = jnp.zeros_like(sums)
    stack[...] = jnp.zeros_like(stack)

    for copy in small_copies():
        copy.wait()

    lane = lax.broadcasted_iota(jnp.int32, (dates, devices), 1)
    date = lax.broadcasted_iota(jnp.int32, (dates, devices), 0)
    scales = []
    for upper in range(2):
        chosen_date = lane == date + (plane - 1 + upper) * BAND
        scales.append(
            jnp.sum(jnp.where(chosen_date, baseline[...], 0.0), axis=1, keepdims=True)
        )

    owner = pair_owner[...]
    pairs = owner.shape[1]
    down = lax.broadcasted_iota(jnp.int32, (pairs, pairs), 0)
    across = lax.broadcasted_iota(jnp.int32, (pairs, pairs), 1)
    owner_column = jnp.sum(jnp.where(down == across, owner, 0), axis=1, keepdims=True)
    earlier = (owner_column == owner) & (down < across)
    slot_of = owner * CAP + jnp.sum(jnp.where(earlier, 1, 0), axis=0, keepdims=True)
    first, second = pair_list[0:1, :], pair_list[1:2, :]
    distance = second - first
    first_here = lax.div(first, BAND) == plane
    second_here = lax.div(second, BAND) == plane
    first_at = lax.rem(first, BAND)
    second_at = lax.rem(second, BAND)
    others = (QUANTITIES - 1) * TILE
    places = (
        (first_here, first_at + distance * TILE),
        (first_here, first_at + (BAND + distance) * TILE),
        (second_here, second_at + distance * TILE + BAND),
        (second_here, second_at + (BAND + distance) * TILE + BAND),
        (first_here, first_at),
        (second_here, jnp.where(first_here, first_at + BAND, others + first_at)),
        (first_here, jnp.where(second_here, second_at, others + second_at + BAND)),
        (second_here, second_at + BAND),
    )
    total = devices * len(places) * CAP
    line = lax.broadcasted_iota(jnp.int32, (total, pairs), 0)
    part = (line & (len(places) * CAP - 1)) - (line & (CAP - 1))
    taken = lax.div(line, len(places)) - lax.div(line & (len(places) * CAP - 1), len(places)) + (line & (CAP - 1)) == slot_of
    listed = jnp.full((total, pairs), -1, jnp.int32)
    for at, (valid, value) in enumerate(places):
        listed = jnp.where(taken & valid & (part == at * CAP), value, listed)
    listed = jnp.max(listed.astype(jnp.float32), axis=1, keepdims=True)
    depth = lax.broadcasted_iota(jnp.int32, (total, DEPTH), 1).astype(jnp.float32)
    hit = (depth == listed)
    for piece in range(1, PIECES):
        hit = hit | (depth == listed + piece * UNIT)
    picks[...] = jnp.where(hit & (listed >= 0.0), 1.0, 0.0).astype(jnp.bfloat16)

    def forward(chunk):
        @pl.when(chunk + AHEAD < chunks)
        def _():
            own_relays(chunk + AHEAD)

        for step in (1, 2, 3):
            for upper in range(2):
                plane_arrival(step, upper, chunk).wait_recv()

                @pl.when(relays[upper])
                def _():
                    which = spot ^ step
                    relay_copy(
                        upper, chunk, which, place(upper, chunk, own_slot(upper, which))
                    ).start()

    own_rows = lax.broadcasted_iota(jnp.int32, (dates, LANES), 0) < BAND

    def compute(chunk):
        for upper in range(2):
            own_copy(upper, chunk).wait()

            @pl.when(gets_relays[upper])
            def _():
                relay_all(upper, chunk).wait_recv()

        phase = lax.div(chunk, steps)
        tile = lax.div(phase, HALVES)
        step = lax.rem(chunk, steps)

        @pl.loop(0, WIDE)
        def _(block):
            column = pl.multiple_of(
                (lax.rem(phase, HALVES) * (steps * WIDE) + step * WIDE + block) * LANES, LANES
            )
            totals = []
            for look_row in range(look_rows):
                found = [None] * QUANTITIES

                def add(at, value):
                    found[at] = value if found[at] is None else found[at] + value

                for row in range(LOOK_ROWS):
                    flat = []
                    for upper in range(2):
                        source = (upper * tiles + tile) * look_rows + look_row
                        level = heights[source, row:row + 1, pl.ds(column, LANES)]
                        cosine, sine = cos_sin(scales[upper] * level)
                        at = pl.ds(look_row * LOOK_ROWS + row, dates, stride=TILE)
                        real = window[upper, chunk, 0, block, at, :]
                        imag = window[upper, chunk, 1, block, at, :]
                        flat.append((real * cosine - imag * sine, real * sine + imag * cosine))
                    own_real, own_imag = (jnp.where(own_rows, u, l) for l, u in zip(*flat))
                    add(0, own_real * own_real + own_imag * own_imag)
                    rest_real, rest_imag = (jnp.where(own_rows, l, u) for l, u in zip(*flat))
                    add(QUANTITIES - 1, rest_real * rest_real + rest_imag * rest_imag)
                    for distance in range(1, BAND + 1):
                        other_real, other_imag = (
                            jnp.where(
                                own_rows, pltpu.roll(u, dates - distance, 0), pltpu.roll(l, distance, 0)
                            )
                            for l, u in zip(*flat)
                        )
                        add(distance, own_real * other_real + own_imag * other_imag)
                        add(BAND + distance, own_imag * other_real - own_real * other_imag)
                totals.append(jnp.concatenate(found, axis=0))
            weights = box[
                pl.ds(pl.multiple_of((step * WIDE + block) * look_rows * LANES, LANES), look_rows * LANES), :
            ]
            summed = sums[phase]
            for piece in split(jnp.concatenate(totals, axis=1), 2):
                summed = summed + jnp.dot(piece, weights, preferred_element_type=jnp.float32)
            sums[phase] = summed

    def done(step):
        return jnp.maximum(0, jnp.minimum(2 * (step - START), step - LAG))

    @pl.loop(0, chunks + LAG)
    def _(step):
        @pl.when(step < chunks)
        def _():
            forward(step)

        @pl.when(step == START)
        def _():
            @pl.loop(0, planes)
            def _(source):
                height_arrival(source).wait_recv()

        @pl.loop(done(step), done(step + 1))
        def _(chunk):
            compute(chunk)

    line = lax.broadcasted_iota(jnp.int32, (UNIT, LANES), 0)
    turned = (line >= (1 + BAND) * TILE) & (line < (1 + 2 * BAND) * TILE) & ((line & BAND) == BAND)
    scale = jnp.where(turned, -1.0, 1.0) * (1.0 / (LOOK_ROWS * LOOK_COLS))
    size = len(places) * CAP
    for tile in range(tiles):
        for half in range(HALVES):
            for at, piece in enumerate(split(sums[tile * HALVES + half] * scale, PIECES)):
                stack[at * UNIT:(at + 1) * UNIT, half * LANES:(half + 1) * LANES] = piece
        chosen[...] = jnp.dot(picks[...], stack[...], preferred_element_type=jnp.float32)

        @pl.loop(0, devices // BAND)
        def _(some):
            for one in range(BAND):
                which = some * BAND + one
                for half in range(HALVES):
                    near, far_side, first_power, second_power = (
                        chosen[
                            pl.ds(pl.multiple_of(which * size + at * TILE, TILE), TILE),
                            half * LANES:(half + 1) * LANES,
                        ]
                        for at in range(4)
                    )
                    squares = [v * v for v in (near, far_side)]
                    squares = [v + pltpu.roll(v, CAP, 0) for v in squares]
                    level = jnp.sqrt(jnp.where(own_rows, squares[0], squares[1]))
                    ratio = level / jnp.sqrt((first_power + EPSILON) * (second_power + EPSILON))
                    for at, value in enumerate((near, far_side, ratio)):
                        outbox[which, (tile * HALVES + half) * 3 + at] = value

    def peer(step):
        return lax.rem(me + step, devices)

    def out_copy(to):
        return pltpu.make_async_remote_copy(
            src_ref=outbox.at[to],
            dst_ref=inbox.at[me],
            send_sem=out_send.at[to],
            recv_sem=out_recv.at[me],
            device_id={"date": to},
        )

    def out_arrival(source):
        return pltpu.make_async_remote_copy(
            src_ref=outbox.at[source],
            dst_ref=inbox.at[source],
            send_sem=out_send.at[source],
            recv_sem=out_recv.at[source],
            device_id={"date": source},
        )

    @pl.loop(1, devices)
    def _(step):
        out_copy(peer(step)).start()

    inbox[me] = outbox[me]

    @pl.loop(0, planes)
    def _(to_plane):
        @pl.when(to_plane * BAND + reader != me)
        def _():
            height_copy(to_plane).wait_send()

    @pl.loop(0, chunks)
    def _(chunk):
        for upper in range(2):
            plane_all(upper, chunk).wait_send()

            @pl.when(relays[upper])
            def _():
                relay_all(upper, chunk).wait_send()

    @pl.loop(1, devices)
    def _(step):
        out_arrival(peer(step)).wait_recv()

    looks = coherence_out.shape[0] // CAP
    left = lax.broadcasted_iota(jnp.int32, (TILE, LANES), 1) < part_lanes
    for quarter in range(BAND):
        for tile in range(tiles):
            for part in range(3):
                sides = []
                for half in range(HALVES):
                    at = (tile * HALVES + half) * 3 + part
                    value = inbox[quarter, at]
                    for other in range(1, planes):
                        value = value + inbox[other * BAND + quarter, at]
                    sides.append(value)
                here, there = sides
                values = (
                    jnp.where(left, here, pltpu.roll(there, part_lanes, 1)),
                    jnp.where(left, pltpu.roll(here, part_lanes, 1), there),
                )
                for look_row, value in enumerate(values):
                    for c in range(2):
                        upper = 1 - part if part < 2 else 1 - c
                        at = ((quarter * 2 + upper) * tiles + tile) * look_rows + look_row
                        piece = value[c * CAP:(c + 1) * CAP]
                        if part < 2:
                            looks_out[pl.ds(c * looks + at, CAP, stride=2 * looks), :] = piece
                        else:
                            coherence_out[pl.ds(at, CAP, stride=looks), :] = piece

    @pl.loop(1, devices)
    def _(step):
        out_copy(peer(step)).wait_send()


def body(images, height_phase, baseline, pair_list, pair_owner):
    devices = lax.axis_size("date")
    rows, columns = images.shape[2:]
    lanes = columns // LOOK_COLS
    looks = rows // LOOK_ROWS
    planes = devices // BAND
    tiles = rows // (2 * BAND * TILE)
    phases = tiles * HALVES
    chunks = phases * (columns // (HALVES * LANES * WIDE))
    dates = 2 * BAND
    pairs = pair_list.shape[0]
    assert lanes == LANES and rows == LOOK_ROWS * devices and TILE == 2 * LOOK_ROWS and HALVES == 2
    assert rows % (2 * BAND * TILE) == 0 and columns % (HALVES * LANES * WIDE) == 0
    assert PIECES * UNIT <= DEPTH
    vmem = pl.BlockSpec(memory_space=pltpu.VMEM)
    hbm = pl.BlockSpec(memory_space=pltpu.HBM)
    dma = pltpu.SemaphoreType.DMA
    tiled = images[0].reshape(2, rows // TILE, TILE, columns // LANES, LANES).transpose(0, 1, 3, 2, 4)
    inputs = [
        pltpu.with_memory_space_constraint(v, pltpu.HBM)
        for v in (tiled, height_phase, baseline[None], pair_list.T, pair_owner.T)
    ]
    scratch = [
        pltpu.VMEM((2, chunks, 2, WIDE, dates * TILE, LANES), jnp.float32),
        pltpu.VMEM((planes, LOOK_ROWS, columns), jnp.float32),
        pltpu.VMEM((2 * columns // HALVES, lanes), jnp.bfloat16),
        pltpu.VMEM((phases, UNIT, lanes), jnp.float32),
        pltpu.VMEM((devices * TILE * CAP, DEPTH), jnp.bfloat16),
        pltpu.VMEM((DEPTH, HALVES * lanes), jnp.bfloat16),
        pltpu.VMEM((devices * TILE * CAP, HALVES * lanes), jnp.float32),
        pltpu.VMEM((devices, phases * 3, TILE, lanes), jnp.float32),
        pltpu.VMEM((devices, phases * 3, TILE, lanes), jnp.float32),
        pltpu.VMEM((1, devices), jnp.float32),
        pltpu.VMEM((2, pairs), jnp.int32),
        pltpu.VMEM((1, pairs), jnp.int32),
    ]
    size = sum(math.prod(s.shape) * jnp.dtype(s.dtype).itemsize for s in scratch)
    scratch += [
        pltpu.SemaphoreType.REGULAR((planes - 1,)),
        dma((3,)),
        dma((2, chunks)),
        dma((2, chunks)),
        dma((2, chunks, BAND)),
        dma((2, chunks)),
        dma((planes,)),
        dma((planes,)),
        dma((devices,)),
        dma((devices,)),
    ]
    look, coherence = pl.pallas_call(
        functools.partial(kernel, devices, phases),
        out_shape=(
            jax.ShapeDtypeStruct((CAP * 2 * looks, lanes), jnp.float32),
            jax.ShapeDtypeStruct((CAP * looks, lanes), jnp.float32),
        ),
        in_specs=[hbm] * 5,
        out_specs=(vmem, vmem),
        scratch_shapes=scratch,
        compiler_params=pltpu.CompilerParams(
            collective_id=0, has_side_effects=True, vmem_limit_bytes=size + (6 << 20)
        ),
    )(*inputs)
    return look.reshape(CAP, 2, looks, lanes), coherence.reshape(CAP, looks, lanes)


def solution(mesh):
    in_specs = (
        P(("groups", "date"), None, None, None),
        P(("groups", "date"), None),
        P("groups"),
        P(),
        P(),
    )
    out_specs = (P(("groups", "date"), None, None, None), P(("groups", "date"), None, None))
    return jax.shard_map(body, mesh=mesh, in_specs=in_specs, out_specs=out_specs, check_vma=False)
```

time: 42.9 us -> 38.8 us (0.904)
  Pallas kernels: 38.8 us -> 36.6 us
  local copies, waits for them, and re-layouts: 2.85 us -> 1.25 us
    pallas_call x1, Pallas kernels: 38.8 us -> 36.6 us  [body(): pl.pallas_call(functools.partial(kernel, devices, phases), out_shape=(jax...]
    unnamed x2, local copies, waits for them, and re-layouts: 2.85 us -> 1.25 us
where the time goes in v1:
time: 38.8 us; the launch traced here: 38.5 us
  Pallas kernels  36.6 us (94%)
  local copies, waits for them, and re-layouts  1.25 us (3%)
  between operations  0.64 us (2%)
    pallas_call x1, Pallas kernels, body(): pl.pallas_call(functools.partial(kernel, devices, phases), out_shape=(jax...  36.6 us
    unnamed x2, local copies, waits for them, and re-layouts  1.25 us

profile of v1, /device:TPU:1, one launch (start us, length us, event | category | flops | bytes accessed | tf_op | source)
XLA Modules:
  0.0 38.5 jit_solution(1055543748194396096)
XLA Ops:
  0.6 36.6 %shard_map.68 = (f32[128,128]{1,0:T(8,128)S(1)}, f32[64,128]{1,0:T(8,128)S(1)}) custom-call(f32[2,8,20,8,128]{4,3,2,1,0:T(8,128)} %bitcast.10, f32[4,2560]{1,0:T(4,128)} %height.1, f32[1,16]{1,0:T(1,128)} %bitcast.12, s32[2,32]{1,0:T(2,128)} %bitcast.11, s32[1,32]{1,0:T(1,128)} %bitcast.13), custom_call_target="tpu_custom_call" | custom-call | tf_op jit(solution)/shard_map/pallas_call | solution.py:560
  37.2 0.6 %copy.9 = f32[4,2,16,128]{3,2,1,0:T(8,128)} copy(f32[4,2,16,128]{3,2,1,0:T(8,128)S(1)} %bitcast.8) | data formatting | bytes 131072
  37.8 0.6 %copy.10 = f32[4,16,128]{2,1,0:T(8,128)} copy(f32[4,16,128]{2,1,0:T(8,128)S(1)} %bitcast.9) | data formatting | bytes 65536

commit v2 on v1

--- a/solution.py
+++ b/solution.py
@@ -18,7 +18,9 @@
 HALVES = 2
 WIDE = 2
 QUANTITIES = 2 + 2 * BAND
-UNIT = QUANTITIES * TILE
+LINES = QUANTITIES * TILE
+UNIT = LINES - TILE
+PARTS = 8
 PIECES = 3
 DEPTH = 256
 AHEAD = 3
@@ -50,8 +52,14 @@
 def kernel(
     devices, phases, images, height, baseline_in, pair_list_in, pair_owner_in, looks_out, coherence_out,
     window, heights, box, sums, picks, stack, chosen, outbox, inbox, baseline, pair_list, pair_owner,
-    far, small_sem, plane_send, relay_send, plane_recv, relay_recv, height_send, height_recv, out_send, out_recv,
+    table, index, staged, plane_inbox, *rest,
 ):
+    early = phases - 1
+    units, outboxes = rest[:early], rest[early:2 * early]
+    (
+        far, small_sem, plane_send, relay_send, plane_recv, relay_recv, height_send, height_recv,
+        unit_send, unit_recv, slot_send, slot_recv, out_send, out_recv,
+    ) = rest[2 * early:]
     me = lax.axis_index("date")
     planes = devices // BAND
     plane = lax.div(me, BAND)
@@ -305,8 +313,35 @@
     depth = lax.broadcasted_iota(jnp.int32, (total, DEPTH), 1).astype(jnp.float32)
     hit = (depth == listed)
     for piece in range(1, PIECES):
-        hit = hit | (depth == listed + piece * UNIT)
+        hit = hit | (depth == listed + piece * LINES)
     picks[...] = jnp.where(hit & (listed >= 0.0), 1.0, 0.0).astype(jnp.bfloat16)
+
+    first_line = lax.div(first, BAND) * UNIT + first_at
+    second_line = lax.div(second, BAND) * UNIT + second_at
+    lines_of = (
+        first_line + distance * TILE,
+        first_line + (BAND + distance) * TILE,
+        second_line + distance * TILE + BAND,
+        second_line + (BAND + distance) * TILE + BAND,
+        first_line,
+        first_line + BAND,
+        second_line,
+        second_line + BAND,
+    )
+    slots = BAND * CAP
+    empty = planes * UNIT
+    slot = lax.broadcasted_iota(jnp.int32, (slots, pairs), 0) + plane * slots
+    taken = slot == slot_of
+    table_lane = lax.broadcasted_iota(jnp.int32, (slots, LANES), 1)
+    entries = jnp.zeros((slots, LANES), jnp.int32)
+    for at, value in enumerate(lines_of):
+        listed = empty + jnp.sum(jnp.where(taken, value - empty, 0), axis=1, keepdims=True)
+        entries = jnp.where(table_lane == at, listed, entries)
+    table[...] = jnp.clip(entries, 0, empty)
+    index_copy = pltpu.make_async_copy(table, index, small_sem.at[3])
+    index_copy.start()
+    for unit in units:
+        unit[empty:, :] = jnp.zeros((TILE, LANES), jnp.float32)
 
     def forward(chunk):
         @pl.when(chunk + AHEAD < chunks)
@@ -382,8 +417,95 @@
                 summed = summed + jnp.dot(piece, weights, preferred_element_type=jnp.float32)
             sums[phase] = summed
 
+    line = lax.broadcasted_iota(jnp.int32, (LINES, LANES), 0)
+    turned = (line >= (1 + BAND) * TILE) & (line < (1 + 2 * BAND) * TILE) & ((line & BAND) == BAND)
+    scale = jnp.where(turned, -1.0, 1.0) * (1.0 / (LOOK_ROWS * LOOK_COLS))
+
+    def unit_lines(phase, which):
+        return units[phase].at[pl.ds(pl.multiple_of(which * UNIT, TILE), UNIT), :]
+
+    def unit_copy(phase, to_plane):
+        return pltpu.make_async_remote_copy(
+            src_ref=unit_lines(phase, plane),
+            dst_ref=unit_lines(phase, plane),
+            send_sem=unit_send.at[phase, to_plane],
+            recv_sem=unit_recv.at[phase, plane],
+            device_id={"date": to_plane * BAND + spot},
+        )
+
+    def unit_arrival(phase, source):
+        return pltpu.make_async_remote_copy(
+            src_ref=unit_lines(phase, source),
+            dst_ref=unit_lines(phase, source),
+            send_sem=unit_send.at[phase, source],
+            recv_sem=unit_recv.at[phase, source],
+            device_id={"date": source * BAND + spot},
+        )
+
+    def other_plane(turn):
+        return lax.rem(plane + turn, planes)
+
+    def unit_start(phase):
+        units[phase][pl.ds(pl.multiple_of(plane * UNIT, TILE), UNIT), :] = sums[phase, :UNIT] * scale[:UNIT]
+
+        @pl.loop(1, planes)
+        def _(turn):
+            unit_copy(phase, other_plane(turn)).start()
+
+    def ratio_of(near, far_side, first_power, second_power):
+        squares = [v * v for v in (near, far_side)]
+        squares = [v + pltpu.roll(v, CAP, 0) for v in squares]
+        level = jnp.sqrt(jnp.where(own_rows, squares[0], squares[1]))
+        return level / jnp.sqrt((first_power + EPSILON) * (second_power + EPSILON))
+
+    def parcel(to):
+        return pl.ds(pl.multiple_of(to * 3 * TILE, TILE), 3 * TILE)
+
+    def slot_copy(phase, to):
+        return pltpu.make_async_remote_copy(
+            src_ref=outboxes[phase].at[parcel(to), :],
+            dst_ref=plane_inbox.at[phase, spot],
+            send_sem=slot_send.at[phase, to],
+            recv_sem=slot_recv.at[phase, spot],
+            device_id={"date": plane * BAND + to},
+        )
+
+    def slot_arrival(phase, source):
+        return pltpu.make_async_remote_copy(
+            src_ref=outboxes[phase].at[parcel(source), :],
+            dst_ref=plane_inbox.at[phase, source],
+            send_sem=slot_send.at[phase, source],
+            recv_sem=slot_recv.at[phase, source],
+            device_id={"date": plane * BAND + source},
+        )
+
+    def choose(phase):
+        unit = units[phase]
+        for which in range(BAND):
+            for at in range(CAP):
+                for part in range(PARTS):
+                    line = jnp.clip(index[which * CAP + at, part], 0, planes * UNIT)
+                    row = (which * 4 + part // 2) * TILE + part % 2 * CAP + at
+                    staged[phase, row:row + 1, :] = unit[pl.ds(line, 1), :]
+        for which in range(BAND):
+            near, far_side, first_power, second_power = (
+                staged[phase, (which * 4 + at) * TILE:(which * 4 + at + 1) * TILE, :] for at in range(4)
+            )
+            ratio = ratio_of(near, far_side, first_power, second_power)
+            outboxes[phase][which * 3 * TILE:(which + 1) * 3 * TILE, :] = jnp.concatenate(
+                [near, far_side, ratio], axis=0
+            )
+        for step in (2, 3, 1):
+            slot_copy(phase, spot ^ step).start()
+        plane_inbox[phase, spot] = outboxes[phase][parcel(spot), :]
+
+    index_copy.wait()
+
     def done(step):
         return jnp.maximum(0, jnp.minimum(2 * (step - START), step - LAG))
+
+    def ready(phase):
+        return max((phase + 1) * steps + LAG - 1, -(-(phase + 1) * steps // 2) + START - 1)
 
     @pl.loop(0, chunks + LAG)
     def _(step):
@@ -401,34 +523,25 @@
         def _(chunk):
             compute(chunk)
 
-    line = lax.broadcasted_iota(jnp.int32, (UNIT, LANES), 0)
-    turned = (line >= (1 + BAND) * TILE) & (line < (1 + 2 * BAND) * TILE) & ((line & BAND) == BAND)
-    scale = jnp.where(turned, -1.0, 1.0) * (1.0 / (LOOK_ROWS * LOOK_COLS))
+        for phase in range(early):
+            @pl.when(step == ready(phase))
+            def _():
+                unit_start(phase)
+
     size = len(places) * CAP
-    for tile in range(tiles):
-        for half in range(HALVES):
-            for at, piece in enumerate(split(sums[tile * HALVES + half] * scale, PIECES)):
-                stack[at * UNIT:(at + 1) * UNIT, half * LANES:(half + 1) * LANES] = piece
-        chosen[...] = jnp.dot(picks[...], stack[...], preferred_element_type=jnp.float32)
-
-        @pl.loop(0, devices // BAND)
-        def _(some):
-            for one in range(BAND):
-                which = some * BAND + one
-                for half in range(HALVES):
-                    near, far_side, first_power, second_power = (
-                        chosen[
-                            pl.ds(pl.multiple_of(which * size + at * TILE, TILE), TILE),
-                            half * LANES:(half + 1) * LANES,
-                        ]
-                        for at in range(4)
-                    )
-                    squares = [v * v for v in (near, far_side)]
-                    squares = [v + pltpu.roll(v, CAP, 0) for v in squares]
-                    level = jnp.sqrt(jnp.where(own_rows, squares[0], squares[1]))
-                    ratio = level / jnp.sqrt((first_power + EPSILON) * (second_power + EPSILON))
-                    for at, value in enumerate((near, far_side, ratio)):
-                        outbox[which, (tile * HALVES + half) * 3 + at] = value
+    for at, piece in enumerate(split(sums[early] * scale, PIECES)):
+        stack[at * LINES:(at + 1) * LINES, :] = piece
+    chosen[...] = jnp.dot(picks[...], stack[...], preferred_element_type=jnp.float32)
+
+    @pl.loop(0, devices // BAND)
+    def _(some):
+        for one in range(BAND):
+            which = some * BAND + one
+            near, far_side, first_power, second_power = (
+                chosen[pl.ds(pl.multiple_of(which * size + at * TILE, TILE), TILE), :] for at in range(4)
+            )
+            for at, value in enumerate((near, far_side, ratio_of(near, far_side, first_power, second_power))):
+                outbox[which, at] = value
 
     def peer(step):
         return lax.rem(me + step, devices)
@@ -457,6 +570,13 @@
 
     inbox[me] = outbox[me]
 
+    for phase in range(early):
+        @pl.loop(1, planes)
+        def _(turn):
+            unit_arrival(phase, other_plane(turn)).wait_recv()
+
+        choose(phase)
+
     @pl.loop(0, planes)
     def _(to_plane):
         @pl.when(to_plane * BAND + reader != me)
@@ -471,6 +591,10 @@
             @pl.when(relays[upper])
             def _():
                 relay_all(upper, chunk).wait_send()
+
+    for phase in range(early):
+        for step in range(1, BAND):
+            slot_arrival(phase, spot ^ step).wait_recv()
 
     @pl.loop(1, devices)
     def _(step):
@@ -483,11 +607,14 @@
             for part in range(3):
                 sides = []
                 for half in range(HALVES):
-                    at = (tile * HALVES + half) * 3 + part
-                    value = inbox[quarter, at]
-                    for other in range(1, planes):
-                        value = value + inbox[other * BAND + quarter, at]
-                    sides.append(value)
+                    phase = tile * HALVES + half
+                    if phase < early:
+                        sides.append(plane_inbox[phase, quarter, part * TILE:(part + 1) * TILE, :])
+                    else:
+                        value = inbox[quarter, part]
+                        for other in range(1, planes):
+                            value = value + inbox[other * BAND + quarter, part]
+                        sides.append(value)
                 here, there = sides
                 values = (
                     jnp.where(left, here, pltpu.roll(there, part_lanes, 1)),
@@ -503,6 +630,14 @@
                         else:
                             coherence_out[pl.ds(at, CAP, stride=looks), :] = piece
 
+    for phase in range(early):
+        @pl.loop(1, planes)
+        def _(turn):
+            unit_copy(phase, other_plane(turn)).wait_send()
+
+        for step in range(1, BAND):
+            slot_copy(phase, spot ^ step).wait_send()
+
     @pl.loop(1, devices)
     def _(step):
         out_copy(peer(step)).wait_send()
@@ -516,12 +651,13 @@
     planes = devices // BAND
     tiles = rows // (2 * BAND * TILE)
     phases = tiles * HALVES
+    early = phases - 1
     chunks = phases * (columns // (HALVES * LANES * WIDE))
     dates = 2 * BAND
     pairs = pair_list.shape[0]
     assert lanes == LANES and rows == LOOK_ROWS * devices and TILE == 2 * LOOK_ROWS and HALVES == 2
     assert rows % (2 * BAND * TILE) == 0 and columns % (HALVES * LANES * WIDE) == 0
-    assert PIECES * UNIT <= DEPTH
+    assert PIECES * LINES <= DEPTH
     vmem = pl.BlockSpec(memory_space=pltpu.VMEM)
     hbm = pl.BlockSpec(memory_space=pltpu.HBM)
     dma = pltpu.SemaphoreType.DMA
@@ -534,26 +670,36 @@
         pltpu.VMEM((2, chunks, 2, WIDE, dates * TILE, LANES), jnp.float32),
         pltpu.VMEM((planes, LOOK_ROWS, columns), jnp.float32),
         pltpu.VMEM((2 * columns // HALVES, lanes), jnp.bfloat16),
-        pltpu.VMEM((phases, UNIT, lanes), jnp.float32),
+        pltpu.VMEM((phases, LINES, lanes), jnp.float32),
         pltpu.VMEM((devices * TILE * CAP, DEPTH), jnp.bfloat16),
-        pltpu.VMEM((DEPTH, HALVES * lanes), jnp.bfloat16),
-        pltpu.VMEM((devices * TILE * CAP, HALVES * lanes), jnp.float32),
-        pltpu.VMEM((devices, phases * 3, TILE, lanes), jnp.float32),
-        pltpu.VMEM((devices, phases * 3, TILE, lanes), jnp.float32),
+        pltpu.VMEM((DEPTH, lanes), jnp.bfloat16),
+        pltpu.VMEM((devices * TILE * CAP, lanes), jnp.float32),
+        pltpu.VMEM((devices, 3, TILE, lanes), jnp.float32),
+        pltpu.VMEM((devices, 3, TILE, lanes), jnp.float32),
         pltpu.VMEM((1, devices), jnp.float32),
         pltpu.VMEM((2, pairs), jnp.int32),
         pltpu.VMEM((1, pairs), jnp.int32),
+        pltpu.VMEM((BAND * CAP, LANES), jnp.int32),
+        pltpu.SMEM((BAND * CAP, LANES), jnp.int32),
+        pltpu.VMEM((early, BAND * 4 * TILE, lanes), jnp.float32),
+        pltpu.VMEM((early, BAND, 3 * TILE, lanes), jnp.float32),
     ]
+    scratch += [pltpu.VMEM((planes * UNIT + TILE, lanes), jnp.float32)] * early
+    scratch += [pltpu.VMEM((BAND * 3 * TILE, lanes), jnp.float32)] * early
     size = sum(math.prod(s.shape) * jnp.dtype(s.dtype).itemsize for s in scratch)
     scratch += [
         pltpu.SemaphoreType.REGULAR((planes - 1,)),
-        dma((3,)),
+        dma((4,)),
         dma((2, chunks)),
         dma((2, chunks)),
         dma((2, chunks, BAND)),
         dma((2, chunks)),
         dma((planes,)),
         dma((planes,)),
+        dma((early, planes)),
+        dma((early, planes)),
+        dma((early, BAND)),
+        dma((early, BAND)),
         dma((devices,)),
         dma((devices,)),
     ]

time: 38.8 us -> 36.2 us (0.933)
  Pallas kernels: 36.6 us -> 34.1 us
    pallas_call x1, Pallas kernels: 36.6 us -> 34.1 us  [body(): pl.pallas_call(functools.partial(kernel, devices, phases), out_shape=(jax...]
where the time goes in v2:
time: 36.2 us; the launch traced here: 36 us
  Pallas kernels  34.1 us (94%)
  local copies, waits for them, and re-layouts  1.25 us (3%)
  between operations  0.64 us (2%)
    pallas_call x1, Pallas kernels, body(): pl.pallas_call(functools.partial(kernel, devices, phases), out_shape=(jax...  34.1 us
    unnamed x2, local copies, waits for them, and re-layouts  1.25 us

profile of v2, /device:TPU:1, one launch (start us, length us, event | category | flops | bytes accessed | tf_op | source)
XLA Modules:
  0.0 36.0 jit_solution(14959904002055998596)
XLA Ops:
  0.6 34.1 %shard_map.68 = (f32[128,128]{1,0:T(8,128)S(1)}, f32[64,128]{1,0:T(8,128)S(1)}) custom-call(f32[2,8,20,8,128]{4,3,2,1,0:T(8,128)} %bitcast.10, f32[4,2560]{1,0:T(4,128)} %height.1, f32[1,16]{1,0:T(1,128)} %bitcast.12, s32[2,32]{1,0:T(2,128)} %bitcast.11, s32[1,32]{1,0:T(1,128)} %bitcast.13), custom_call_target="tpu_custom_call" | custom-call | tf_op jit(solution)/shard_map/pallas_call | solution.py:706
  34.8 0.6 %copy.9 = f32[4,2,16,128]{3,2,1,0:T(8,128)} copy(f32[4,2,16,128]{3,2,1,0:T(8,128)S(1)} %bitcast.8) | data formatting | bytes 131072
  35.4 0.6 %copy.10 = f32[4,16,128]{2,1,0:T(8,128)} copy(f32[4,16,128]{2,1,0:T(8,128)S(1)} %bitcast.9) | data formatting | bytes 65536

commit v3 on v2

--- a/solution.py
+++ b/solution.py
@@ -16,17 +16,14 @@
 LANES = 128
 TILE = 8
 HALVES = 2
-WIDE = 2
 QUANTITIES = 2 + 2 * BAND
 LINES = QUANTITIES * TILE
 UNIT = LINES - TILE
 PARTS = 8
 PIECES = 3
 DEPTH = 256
-AHEAD = 3
-FIRST = 2
-START = 6
-LAG = 5
+FIRST = 1
+LAG = 3
 
 
 def split(values, parts):
@@ -49,6 +46,17 @@
     return cosine, sine * angle
 
 
+def chunk_list(phases, blocks):
+    chunks = []
+    for phase in range(phases):
+        widths = [blocks - blocks // 2, blocks // 2] if phase < phases - 1 else [blocks - 5, 3, 2]
+        start = phase * blocks
+        for width in widths:
+            chunks.append((start, width))
+            start += width
+    return chunks
+
+
 def kernel(
     devices, phases, images, height, baseline_in, pair_list_in, pair_owner_in, looks_out, coherence_out,
     window, heights, box, sums, picks, stack, chosen, outbox, inbox, baseline, pair_list, pair_owner,
@@ -57,7 +65,7 @@
     early = phases - 1
     units, outboxes = rest[:early], rest[early:2 * early]
     (
-        far, small_sem, plane_send, relay_send, plane_recv, relay_recv, height_send, height_recv,
+        far, small_sem, plane_send, relay_send, plane_recv, relay_recv, height_send, height_recv, height_relay_send,
         unit_send, unit_recv, slot_send, slot_recv, out_send, out_recv,
     ) = rest[2 * early:]
     me = lax.axis_index("date")
@@ -68,8 +76,8 @@
     column_tiles = images.shape[2]
     columns = column_tiles * LANES
     part_columns = columns // HALVES
-    steps = part_columns // (LANES * WIDE)
-    chunks = phases * steps
+    steps = part_columns // LANES
+    chunks = chunk_list(phases, steps)
     side = BAND * TILE
     dates = 2 * BAND
     part_lanes = LANES // HALVES
@@ -92,8 +100,8 @@
     def _():
         hello(me + BAND)
 
-    reader = lax.div(me, planes)
-    own_height = lax.rem(me, planes)
+    reader = spot - lax.rem(spot, look_rows) + lax.rem(plane, 2)
+    own_height = lax.div(plane, 2) * look_rows + lax.rem(spot, look_rows)
 
     def small_copies():
         return [
@@ -124,14 +132,17 @@
             device_id={"date": me},
         )
 
+    def tile_of(quarter, upper, tile):
+        return (quarter >> 1) + 2 * ((quarter & 1) + 2 * (upper * tiles + tile))
+
     def lines(quarter, upper, chunk):
-        phase = lax.div(chunk, steps)
-        tile = (quarter * 2 + upper) * tiles + lax.div(phase, HALVES)
-        column = lax.rem(phase, HALVES) * (steps * WIDE) + lax.rem(chunk, steps) * WIDE
-        return images.at[:, tile, pl.ds(column, WIDE)]
+        start, width = chunks[chunk]
+        tile = tile_of(quarter, upper, start // (steps * HALVES))
+        return images.at[:, tile, start % (steps * HALVES):start % (steps * HALVES) + width]
 
     def place(upper, chunk, slot, size=TILE):
-        return window.at[upper, chunk, :, :, pl.ds(pl.multiple_of(slot * TILE, TILE), size), :]
+        start, width = chunks[chunk]
+        return window.at[upper, :, start:start + width, pl.ds(pl.multiple_of(slot * TILE, TILE), size), :]
 
     def own_slot(upper, which):
         return (1 - upper) * BAND + which
@@ -210,15 +221,18 @@
         for upper in range(2):
             own_copy(upper, chunk).start()
 
-    @pl.loop(0, FIRST)
-    def _(chunk):
+    for chunk in range(FIRST):
         rows_out(chunk)
 
-    @pl.loop(0, AHEAD)
-    def _(chunk):
-        own_relays(chunk)
-
-    for turn in range(planes - 1):
+    def height_direct(to_plane):
+        return (to_plane * BAND + reader != me) & (
+            height_near(to_plane) | ((to_plane > 0) & (to_plane < planes - 1))
+        )
+
+    def height_near(to_plane):
+        return (to_plane - plane < 2) & (plane - to_plane < 2)
+
+    def meet(turn):
         @pl.when(below)
         def _():
             pl.semaphore_signal(far.at[turn], inc=1, device_id={"date": me - BAND})
@@ -229,30 +243,43 @@
 
         pl.semaphore_wait(far.at[turn], jnp.where(below, 1, 0) + jnp.where(above, 1, 0))
 
+    @pl.when(reader == spot)
+    def _():
+        height_own().start()
+
+    meet(0)
+
     @pl.loop(0, planes)
     def _(to_plane):
-        @pl.when(to_plane * BAND + reader != me)
+        @pl.when(height_direct(to_plane) & height_near(to_plane))
         def _():
             height_copy(to_plane).start()
 
-        @pl.when(to_plane * BAND + reader == me)
+    for chunk in range(len(chunks)):
+        own_relays(chunk)
+
+    for turn in range(1, planes - 1):
+        meet(turn)
+
+    @pl.loop(0, planes)
+    def _(to_plane):
+        @pl.when(height_direct(to_plane) & jnp.logical_not(height_near(to_plane)))
         def _():
-            height_own().start()
-
-    @pl.loop(FIRST, chunks)
-    def _(chunk):
+            height_copy(to_plane).start()
+
+    for chunk in range(FIRST, len(chunks)):
         rows_out(chunk)
 
     for upper in range(2):
         @pl.when(jnp.logical_not(gets_relays[upper]))
         def _():
-            @pl.loop(0, chunks)
-            def _(chunk):
-                window[upper, chunk, :, :, upper * side:(upper + 1) * side, :] = jnp.zeros(
-                    (2, WIDE, side, LANES), jnp.float32
+            @pl.loop(0, phases * steps)
+            def _(block):
+                window[upper, :, block, upper * side:(upper + 1) * side, :] = jnp.zeros(
+                    (2, side, LANES), jnp.float32
                 )
 
-    @pl.loop(0, steps * WIDE)
+    @pl.loop(0, steps)
     def _(block):
         shape = (look_rows * LANES, LANES)
         line = lax.broadcasted_iota(jnp.int32, shape, 0)
@@ -344,10 +371,6 @@
         unit[empty:, :] = jnp.zeros((TILE, LANES), jnp.float32)
 
     def forward(chunk):
-        @pl.when(chunk + AHEAD < chunks)
-        def _():
-            own_relays(chunk + AHEAD)
-
         for step in (1, 2, 3):
             for upper in range(2):
                 plane_arrival(step, upper, chunk).wait_recv()
@@ -359,6 +382,30 @@
                         upper, chunk, which, place(upper, chunk, own_slot(upper, which))
                     ).start()
 
+    def height_onward(source, up):
+        origin = lax.div(source, look_rows) * 2 + lax.rem(spot, 2)
+        if up:
+            return (plane == planes - 2) & (origin < planes - 2)
+        return (plane == 1) & (origin > 1)
+
+    def height_relay(source, up):
+        return pltpu.make_async_remote_copy(
+            src_ref=heights.at[source],
+            dst_ref=heights.at[source],
+            send_sem=height_relay_send.at[up, source],
+            recv_sem=height_recv.at[source],
+            device_id={"date": me + BAND * (2 * up - 1)},
+        )
+
+    def height_pass():
+        @pl.loop(0, planes)
+        def _(source):
+            for up in range(2):
+                @pl.when(height_onward(source, up))
+                def _():
+                    height_arrival(source).wait_recv()
+                    height_relay(source, up).start()
+
     own_rows = lax.broadcasted_iota(jnp.int32, (dates, LANES), 0) < BAND
 
     def compute(chunk):
@@ -369,15 +416,13 @@
             def _():
                 relay_all(upper, chunk).wait_recv()
 
-        phase = lax.div(chunk, steps)
-        tile = lax.div(phase, HALVES)
-        step = lax.rem(chunk, steps)
-
-        @pl.loop(0, WIDE)
+        start, width = chunks[chunk]
+
+        @pl.loop(start, start + width)
         def _(block):
-            column = pl.multiple_of(
-                (lax.rem(phase, HALVES) * (steps * WIDE) + step * WIDE + block) * LANES, LANES
-            )
+            phase = lax.div(block, steps)
+            tile = lax.div(phase, HALVES)
+            column = pl.multiple_of(lax.rem(block, steps * HALVES) * LANES, LANES)
             totals = []
             for look_row in range(look_rows):
                 found = [None] * QUANTITIES
@@ -392,8 +437,8 @@
                         level = heights[source, row:row + 1, pl.ds(column, LANES)]
                         cosine, sine = cos_sin(scales[upper] * level)
                         at = pl.ds(look_row * LOOK_ROWS + row, dates, stride=TILE)
-                        real = window[upper, chunk, 0, block, at, :]
-                        imag = window[upper, chunk, 1, block, at, :]
+                        real = window[upper, 0, block, at, :]
+                        imag = window[upper, 1, block, at, :]
                         flat.append((real * cosine - imag * sine, real * sine + imag * cosine))
                     own_real, own_imag = (jnp.where(own_rows, u, l) for l, u in zip(*flat))
                     add(0, own_real * own_real + own_imag * own_imag)
@@ -410,7 +455,7 @@
                         add(BAND + distance, own_imag * other_real - own_real * other_imag)
                 totals.append(jnp.concatenate(found, axis=0))
             weights = box[
-                pl.ds(pl.multiple_of((step * WIDE + block) * look_rows * LANES, LANES), look_rows * LANES), :
+                pl.ds(pl.multiple_of(lax.rem(block, steps) * look_rows * LANES, LANES), look_rows * LANES), :
             ]
             summed = sums[phase]
             for piece in split(jnp.concatenate(totals, axis=1), 2):
@@ -501,32 +546,26 @@
 
     index_copy.wait()
 
-    def done(step):
-        return jnp.maximum(0, jnp.minimum(2 * (step - START), step - LAG))
-
-    def ready(phase):
-        return max((phase + 1) * steps + LAG - 1, -(-(phase + 1) * steps // 2) + START - 1)
-
-    @pl.loop(0, chunks + LAG)
-    def _(step):
-        @pl.when(step < chunks)
-        def _():
-            forward(step)
-
-        @pl.when(step == START)
-        def _():
-            @pl.loop(0, planes)
-            def _(source):
-                height_arrival(source).wait_recv()
-
-        @pl.loop(done(step), done(step + 1))
-        def _(chunk):
-            compute(chunk)
-
-        for phase in range(early):
-            @pl.when(step == ready(phase))
-            def _():
-                unit_start(phase)
+    last = len(chunks) - 1
+    computed = 0
+    for chunk in range(len(chunks) + LAG):
+        if chunk <= last:
+            forward(chunk)
+        if chunk == 0:
+            height_pass()
+        while computed <= min(chunk - LAG, last):
+            if computed == 0:
+                @pl.loop(0, planes)
+                def _(source):
+                    @pl.when(jnp.logical_not(height_onward(source, 0) | height_onward(source, 1)))
+                    def _():
+                        height_arrival(source).wait_recv()
+
+            compute(computed)
+            start, width = chunks[computed]
+            if (start + width) % steps == 0 and computed < last:
+                unit_start(start // steps)
+            computed += 1
 
     size = len(places) * CAP
     for at, piece in enumerate(split(sums[early] * scale, PIECES)):
@@ -579,12 +618,18 @@
 
     @pl.loop(0, planes)
     def _(to_plane):
-        @pl.when(to_plane * BAND + reader != me)
+        @pl.when(height_direct(to_plane))
         def _():
             height_copy(to_plane).wait_send()
 
-    @pl.loop(0, chunks)
-    def _(chunk):
+    @pl.loop(0, planes)
+    def _(source):
+        for up in range(2):
+            @pl.when(height_onward(source, up))
+            def _():
+                height_relay(source, up).wait_send()
+
+    for chunk in range(len(chunks)):
         for upper in range(2):
             plane_all(upper, chunk).wait_send()
 
@@ -623,7 +668,7 @@
                 for look_row, value in enumerate(values):
                     for c in range(2):
                         upper = 1 - part if part < 2 else 1 - c
-                        at = ((quarter * 2 + upper) * tiles + tile) * look_rows + look_row
+                        at = tile_of(quarter, upper, tile) * look_rows + look_row
                         piece = value[c * CAP:(c + 1) * CAP]
                         if part < 2:
                             looks_out[pl.ds(c * looks + at, CAP, stride=2 * looks), :] = piece
@@ -652,11 +697,12 @@
     tiles = rows // (2 * BAND * TILE)
     phases = tiles * HALVES
     early = phases - 1
-    chunks = phases * (columns // (HALVES * LANES * WIDE))
+    blocks = columns // (HALVES * LANES)
+    chunks = len(chunk_list(phases, blocks))
     dates = 2 * BAND
     pairs = pair_list.shape[0]
     assert lanes == LANES and rows == LOOK_ROWS * devices and TILE == 2 * LOOK_ROWS and HALVES == 2
-    assert rows % (2 * BAND * TILE) == 0 and columns % (HALVES * LANES * WIDE) == 0
+    assert rows % (2 * BAND * TILE) == 0 and columns % (HALVES * LANES) == 0 and blocks > 5
     assert PIECES * LINES <= DEPTH
     vmem = pl.BlockSpec(memory_space=pltpu.VMEM)
     hbm = pl.BlockSpec(memory_space=pltpu.HBM)
@@ -667,7 +713,7 @@
         for v in (tiled, height_phase, baseline[None], pair_list.T, pair_owner.T)
     ]
     scratch = [
-        pltpu.VMEM((2, chunks, 2, WIDE, dates * TILE, LANES), jnp.float32),
+        pltpu.VMEM((2, 2, phases * blocks, dates * TILE, LANES), jnp.float32),
         pltpu.VMEM((planes, LOOK_ROWS, columns), jnp.float32),
         pltpu.VMEM((2 * columns // HALVES, lanes), jnp.bfloat16),
         pltpu.VMEM((phases, LINES, lanes), jnp.float32),
@@ -696,6 +742,7 @@
         dma((2, chunks)),
         dma((planes,)),
         dma((planes,)),
+        dma((2, planes)),
         dma((early, planes)),
         dma((early, planes)),
         dma((early, BAND)),

time: 36.2 us -> 34.3 us (0.948)
  Pallas kernels: 34.1 us -> 32.3 us
    pallas_call x1, Pallas kernels: 34.1 us -> 32.3 us  [body(): pl.pallas_call(functools.partial(kernel, devices, phases), out_shape=(jax...]
where the time goes in v3:
time: 34.3 us; the launch traced here: 34.2 us
  Pallas kernels  32.3 us (94%)
  local copies, waits for them, and re-layouts  1.25 us (4%)
  between operations  0.64 us (2%)
    pallas_call x1, Pallas kernels, body(): pl.pallas_call(functools.partial(kernel, devices, phases), out_shape=(jax...  32.3 us
    unnamed x2, local copies, waits for them, and re-layouts  1.25 us

profile of v3, /device:TPU:1, one launch (start us, length us, event | category | flops | bytes accessed | tf_op | source)
XLA Modules:
  0.0 34.2 jit_solution(12280386710267346071)
XLA Ops:
  0.6 32.3 %shard_map.68 = (f32[128,128]{1,0:T(8,128)S(1)}, f32[64,128]{1,0:T(8,128)S(1)}) custom-call(f32[2,8,20,8,128]{4,3,2,1,0:T(8,128)} %bitcast.10, f32[4,2560]{1,0:T(4,128)} %height.1, f32[1,16]{1,0:T(1,128)} %bitcast.12, s32[2,32]{1,0:T(2,128)} %bitcast.11, s32[1,32]{1,0:T(1,128)} %bitcast.13), custom_call_target="tpu_custom_call" | custom-call | tf_op jit(solution)/shard_map/pallas_call | solution.py:753
  32.9 0.6 %copy.9 = f32[4,2,16,128]{3,2,1,0:T(8,128)} copy(f32[4,2,16,128]{3,2,1,0:T(8,128)S(1)} %bitcast.8) | data formatting | bytes 131072
  33.6 0.6 %copy.10 = f32[4,16,128]{2,1,0:T(8,128)} copy(f32[4,16,128]{2,1,0:T(8,128)S(1)} %bitcast.9) | data formatting | bytes 65536

commit v4 on v3

--- a/solution.py
+++ b/solution.py
@@ -57,10 +57,14 @@
     return chunks
 
 
+def tile_of(tiles, quarter, upper, tile):
+    return (quarter >> 1) + 2 * ((quarter & 1) + 2 * (upper * tiles + tile))
+
+
 def kernel(
-    devices, phases, images, height, baseline_in, pair_list_in, pair_owner_in, looks_out, coherence_out,
-    window, heights, box, sums, picks, stack, chosen, outbox, inbox, baseline, pair_list, pair_owner,
-    table, index, staged, plane_inbox, *rest,
+    devices, phases, images, height, baseline_in, pair_list_in, pair_owner_in, inbox, plane_inbox,
+    window, heights, box, sums, picks, stack, chosen, outbox, baseline, pair_list, pair_owner,
+    table, index, staged, *rest,
 ):
     early = phases - 1
     units, outboxes = rest[:early], rest[early:2 * early]
@@ -132,12 +136,9 @@
             device_id={"date": me},
         )
 
-    def tile_of(quarter, upper, tile):
-        return (quarter >> 1) + 2 * ((quarter & 1) + 2 * (upper * tiles + tile))
-
     def lines(quarter, upper, chunk):
         start, width = chunks[chunk]
-        tile = tile_of(quarter, upper, start // (steps * HALVES))
+        tile = tile_of(tiles, quarter, upper, start // (steps * HALVES))
         return images.at[:, tile, start % (steps * HALVES):start % (steps * HALVES) + width]
 
     def place(upper, chunk, slot, size=TILE):
@@ -572,40 +573,44 @@
         stack[at * LINES:(at + 1) * LINES, :] = piece
     chosen[...] = jnp.dot(picks[...], stack[...], preferred_element_type=jnp.float32)
 
+    def peer(step):
+        return lax.rem(me + step, devices)
+
+    def out_copy(to):
+        return pltpu.make_async_remote_copy(
+            src_ref=outbox.at[to],
+            dst_ref=inbox.at[me],
+            send_sem=out_send.at[to],
+            recv_sem=out_recv.at[me],
+            device_id={"date": to},
+        )
+
+    def out_arrival(source):
+        return pltpu.make_async_remote_copy(
+            src_ref=outbox.at[source],
+            dst_ref=inbox.at[source],
+            send_sem=out_send.at[source],
+            recv_sem=out_recv.at[source],
+            device_id={"date": source},
+        )
+
     @pl.loop(0, devices // BAND)
     def _(some):
         for one in range(BAND):
-            which = some * BAND + one
+            which = lax.rem(plane + some, planes) * BAND + one
             near, far_side, first_power, second_power = (
                 chosen[pl.ds(pl.multiple_of(which * size + at * TILE, TILE), TILE), :] for at in range(4)
             )
             for at, value in enumerate((near, far_side, ratio_of(near, far_side, first_power, second_power))):
                 outbox[which, at] = value
 
-    def peer(step):
-        return lax.rem(me + step, devices)
-
-    def out_copy(to):
-        return pltpu.make_async_remote_copy(
-            src_ref=outbox.at[to],
-            dst_ref=inbox.at[me],
-            send_sem=out_send.at[to],
-            recv_sem=out_recv.at[me],
-            device_id={"date": to},
-        )
-
-    def out_arrival(source):
-        return pltpu.make_async_remote_copy(
-            src_ref=outbox.at[source],
-            dst_ref=inbox.at[source],
-            send_sem=out_send.at[source],
-            recv_sem=out_recv.at[source],
-            device_id={"date": source},
-        )
-
-    @pl.loop(1, devices)
-    def _(step):
-        out_copy(peer(step)).start()
+        for one in range(BAND):
+            to = lax.rem(plane + some, planes) * BAND + one
+
+            @pl.when(to != me)
+            def _():
+                out_copy(to).start()
+
 
     inbox[me] = outbox[me]
 
@@ -645,6 +650,24 @@
     def _(step):
         out_arrival(peer(step)).wait_recv()
 
+    for phase in range(early):
+        @pl.loop(1, planes)
+        def _(turn):
+            unit_copy(phase, other_plane(turn)).wait_send()
+
+        for step in range(1, BAND):
+            slot_copy(phase, spot ^ step).wait_send()
+
+    @pl.loop(1, devices)
+    def _(step):
+        out_copy(peer(step)).wait_send()
+
+
+def assemble(planes, phases, inbox, plane_inbox, looks_out, coherence_out):
+    tiles = phases // HALVES
+    early = phases - 1
+    part_lanes = LANES // HALVES
+    look_rows = TILE // LOOK_ROWS
     looks = coherence_out.shape[0] // CAP
     left = lax.broadcasted_iota(jnp.int32, (TILE, LANES), 1) < part_lanes
     for quarter in range(BAND):
@@ -668,24 +691,12 @@
                 for look_row, value in enumerate(values):
                     for c in range(2):
                         upper = 1 - part if part < 2 else 1 - c
-                        at = tile_of(quarter, upper, tile) * look_rows + look_row
+                        at = tile_of(tiles, quarter, upper, tile) * look_rows + look_row
                         piece = value[c * CAP:(c + 1) * CAP]
                         if part < 2:
                             looks_out[pl.ds(c * looks + at, CAP, stride=2 * looks), :] = piece
                         else:
                             coherence_out[pl.ds(at, CAP, stride=looks), :] = piece
-
-    for phase in range(early):
-        @pl.loop(1, planes)
-        def _(turn):
-            unit_copy(phase, other_plane(turn)).wait_send()
-
-        for step in range(1, BAND):
-            slot_copy(phase, spot ^ step).wait_send()
-
-    @pl.loop(1, devices)
-    def _(step):
-        out_copy(peer(step)).wait_send()
 
 
 def body(images, height_phase, baseline, pair_list, pair_owner):
@@ -721,14 +732,12 @@
         pltpu.VMEM((DEPTH, lanes), jnp.bfloat16),
         pltpu.VMEM((devices * TILE * CAP, lanes), jnp.float32),
         pltpu.VMEM((devices, 3, TILE, lanes), jnp.float32),
-        pltpu.VMEM((devices, 3, TILE, lanes), jnp.float32),
         pltpu.VMEM((1, devices), jnp.float32),
         pltpu.VMEM((2, pairs), jnp.int32),
         pltpu.VMEM((1, pairs), jnp.int32),
         pltpu.VMEM((BAND * CAP, LANES), jnp.int32),
         pltpu.SMEM((BAND * CAP, LANES), jnp.int32),
         pltpu.VMEM((early, BAND * 4 * TILE, lanes), jnp.float32),
-        pltpu.VMEM((early, BAND, 3 * TILE, lanes), jnp.float32),
     ]
     scratch += [pltpu.VMEM((planes * UNIT + TILE, lanes), jnp.float32)] * early
     scratch += [pltpu.VMEM((BAND * 3 * TILE, lanes), jnp.float32)] * early
@@ -750,11 +759,11 @@
         dma((devices,)),
         dma((devices,)),
     ]
-    look, coherence = pl.pallas_call(
+    arrived = pl.pallas_call(
         functools.partial(kernel, devices, phases),
         out_shape=(
-            jax.ShapeDtypeStruct((CAP * 2 * looks, lanes), jnp.float32),
-            jax.ShapeDtypeStruct((CAP * looks, lanes), jnp.float32),
+            jax.ShapeDtypeStruct((devices, 3, TILE, lanes), jnp.float32),
+            jax.ShapeDtypeStruct((early, BAND, 3 * TILE, lanes), jnp.float32),
         ),
         in_specs=[hbm] * 5,
         out_specs=(vmem, vmem),
@@ -763,6 +772,16 @@
             collective_id=0, has_side_effects=True, vmem_limit_bytes=size + (6 << 20)
         ),
     )(*inputs)
+    look, coherence = pl.pallas_call(
+        functools.partial(assemble, planes, phases),
+        out_shape=(
+            jax.ShapeDtypeStruct((CAP * 2 * looks, lanes), jnp.float32),
+            jax.ShapeDtypeStruct((CAP * looks, lanes), jnp.float32),
+        ),
+        in_specs=[vmem, vmem],
+        out_specs=(vmem, vmem),
+        compiler_params=pltpu.CompilerParams(vmem_limit_bytes=8 << 20),
+    )(*arrived)
     return look.reshape(CAP, 2, looks, lanes), coherence.reshape(CAP, looks, lanes)
 
 

time: 34.3 us -> 33.6 us (0.980)
  local copies, waits for them, and re-layouts: 1.25 us -> 0 us
  Pallas kernels: 32.3 us -> 32.9 us
    unnamed x2 -> x0, local copies, waits for them, and re-layouts: 1.25 us -> none
    pallas_call x0 -> x1, Pallas kernels: none -> 0.75 us  [body(): pl.pallas_call(functools.partial(assemble, planes, phases), out_shape=(ja...]
where the time goes in v4:
time: 33.6 us; the launch traced here: 33.5 us
  Pallas kernels  32.9 us (98%)
  between operations  0.64 us (2%)
    pallas_call x1, Pallas kernels, body(): pl.pallas_call(functools.partial(kernel, devices, phases), out_shape=(jax...  32.1 us
    pallas_call x1, Pallas kernels, body(): pl.pallas_call(functools.partial(assemble, planes, phases), out_shape=(ja...  0.75 us

profile of v4, /device:TPU:1, one launch (start us, length us, event | category | flops | bytes accessed | tf_op | source)
XLA Modules:
  0.0 33.5 jit_solution(16644952258373140596)
XLA Ops:
  0.6 32.1 %shard_map.68 = (f32[16,3,8,128]{3,2,1,0:T(8,128)S(1)}, f32[1,4,24,128]{3,2,1,0:T(8,128)S(1)}) custom-call(f32[2,8,20,8,128]{4,3,2,1,0:T(8,128)} %bitcast.8, f32[4,2560]{1,0:T(4,128)} %height.1, f32[1,16]{1,0:T(1,128)} %bitcast.10, s32[2,32]{1,0:T(2,128)} %bitcast.9, s32[1,32]{1,0:T(1,128)} %bitcast.11), custom_call_target="tpu_custom_call" | custom-call | tf_op jit(solution)/shard_map/pallas_call | solution.py:762
  32.7 0.7 %shard_map.69 = (f32[128,128]{1,0:T(8,128)}, f32[64,128]{1,0:T(8,128)}) custom-call(f32[16,3,8,128]{3,2,1,0:T(8,128)S(1)} %get-tuple-element.6.inbox, f32[1,4,24,128]{3,2,1,0:T(8,128)S(1)} %get-tuple-element.7.plane_inbox), custom_call_target="tpu_custom_call" | custom-call | tf_op jit(solution)/shard_map/pallas_call | solution.py:775

commit v5 on v4

--- a/solution.py
+++ b/solution.py
@@ -22,7 +22,7 @@
 PARTS = 8
 PIECES = 3
 DEPTH = 256
-FIRST = 1
+FIRST = 2
 LAG = 3
 
 
@@ -35,15 +35,20 @@
     return pieces
 
 
+def horner(square, terms):
+    value = square * terms[-1] + terms[-2]
+    for term in terms[-3::-1]:
+        value = value * square + term
+    return value
+
+
+COSINE = (1, -0.5, 0.041666653, -0.00138887553, 2.47949283e-05, -2.73862867e-07, 1.86794624e-09)
+SINE = (1, -0.166666627, 0.00833326671, -0.000198363021, 2.73895216e-06, -2.24168115e-08)
+
+
 def cos_sin(angle):
     square = angle * angle
-    sine = jnp.full_like(angle, -1.0 / math.factorial(15))
-    for term in range(6, -1, -1):
-        sine = sine * square + (-1.0) ** term / math.factorial(2 * term + 1)
-    cosine = jnp.full_like(angle, 1.0 / math.factorial(16))
-    for term in range(7, -1, -1):
-        cosine = cosine * square + (-1.0) ** term / math.factorial(2 * term)
-    return cosine, sine * angle
+    return horner(square, COSINE), horner(square, SINE) * angle
 
 
 def chunk_list(phases, blocks):

time: 33.6 us -> 33.1 us (0.985)
  Pallas kernels: 32.9 us -> 32.2 us
    pallas_call x1, Pallas kernels: 32.1 us -> 31.4 us  [body(): pl.pallas_call(functools.partial(kernel, devices, phases), out_shape=(jax...]
where the time goes in v5:
time: 33.1 us; the launch traced here: 32.8 us
  Pallas kernels  32.2 us (97%)
  between operations  0.64 us (2%)
    pallas_call x1, Pallas kernels, body(): pl.pallas_call(functools.partial(kernel, devices, phases), out_shape=(jax...  31.4 us
    pallas_call x1, Pallas kernels, body(): pl.pallas_call(functools.partial(assemble, planes, phases), out_shape=(ja...  0.75 us

profile of v5, /device:TPU:1, one launch (start us, length us, event | category | flops | bytes accessed | tf_op | source)
XLA Modules:
  0.0 32.8 jit_solution(6977445989494555503)
XLA Ops:
  0.6 31.4 %shard_map.68 = (f32[16,3,8,128]{3,2,1,0:T(8,128)S(1)}, f32[1,4,24,128]{3,2,1,0:T(8,128)S(1)}) custom-call(f32[2,8,20,8,128]{4,3,2,1,0:T(8,128)} %bitcast.8, f32[4,2560]{1,0:T(4,128)} %height.1, f32[1,16]{1,0:T(1,128)} %bitcast.10, s32[2,32]{1,0:T(2,128)} %bitcast.9, s32[1,32]{1,0:T(1,128)} %bitcast.11), custom_call_target="tpu_custom_call" | custom-call | tf_op jit(solution)/shard_map/pallas_call | solution.py:767
  32.1 0.7 %shard_map.69 = (f32[128,128]{1,0:T(8,128)}, f32[64,128]{1,0:T(8,128)}) custom-call(f32[16,3,8,128]{3,2,1,0:T(8,128)S(1)} %get-tuple-element.6.inbox, f32[1,4,24,128]{3,2,1,0:T(8,128)S(1)} %get-tuple-element.7.plane_inbox), custom_call_target="tpu_custom_call" | custom-call | tf_op jit(solution)/shard_map/pallas_call | solution.py:780

commit v6 on v5

--- a/solution.py
+++ b/solution.py
@@ -54,7 +54,7 @@
 def chunk_list(phases, blocks):
     chunks = []
     for phase in range(phases):
-        widths = [blocks - blocks // 2, blocks // 2] if phase < phases - 1 else [blocks - 5, 3, 2]
+        widths = [blocks - blocks // 2, blocks // 2] if phase < phases - 1 else [blocks - 6, 4, 2]
         start = phase * blocks
         for width in widths:
             chunks.append((start, width))
@@ -424,7 +424,7 @@
 
         start, width = chunks[chunk]
 
-        @pl.loop(start, start + width)
+        @pl.loop(start, start + width, unroll=width == 2)
         def _(block):
             phase = lax.div(block, steps)
             tile = lax.div(phase, HALVES)

time: 33.1 us -> 33.1 us (level)
  no operation moved by 1% of the time
where the time goes in v6:
time: 33.1 us; the launch traced here: 32.8 us
  Pallas kernels  32.2 us (97%)
  between operations  0.64 us (2%)
    pallas_call x1, Pallas kernels, body(): pl.pallas_call(functools.partial(kernel, devices, phases), out_shape=(jax...  31.4 us
    pallas_call x1, Pallas kernels, body(): pl.pallas_call(functools.partial(assemble, planes, phases), out_shape=(ja...  0.75 us

profile of v6, /device:TPU:1, one launch (start us, length us, event | category | flops | bytes accessed | tf_op | source)
XLA Modules:
  0.0 32.8 jit_solution(14215365074271482333)
XLA Ops:
  0.6 31.4 %shard_map.68 = (f32[16,3,8,128]{3,2,1,0:T(8,128)S(1)}, f32[1,4,24,128]{3,2,1,0:T(8,128)S(1)}) custom-call(f32[2,8,20,8,128]{4,3,2,1,0:T(8,128)} %bitcast.8, f32[4,2560]{1,0:T(4,128)} %height.1, f32[1,16]{1,0:T(1,128)} %bitcast.10, s32[2,32]{1,0:T(2,128)} %bitcast.9, s32[1,32]{1,0:T(1,128)} %bitcast.11), custom_call_target="tpu_custom_call" | custom-call | tf_op jit(solution)/shard_map/pallas_call | solution.py:767
  32.0 0.7 %shard_map.69 = (f32[128,128]{1,0:T(8,128)}, f32[64,128]{1,0:T(8,128)}) custom-call(f32[16,3,8,128]{3,2,1,0:T(8,128)S(1)} %get-tuple-element.6.inbox, f32[1,4,24,128]{3,2,1,0:T(8,128)S(1)} %get-tuple-element.7.plane_inbox), custom_call_target="tpu_custom_call" | custom-call | tf_op jit(solution)/shard_map/pallas_call | solution.py:780
